TPU v7x, 32 devices: a whole 2x2x4 slice. The times are simulated.
32 devices in a mesh: groups: 2 (over x), wide: 16 (over z, y, core).
Axes of the slice: x: 2, y: 2, z: 4, core: 2. Of those that a mesh axis runs over, the one named last changes fastest.
Arguments:
- video: bfloat16 [64, 1024, 1152], P(('groups', 'wide')), parts along dimension 0, may hold values from -40 to 40
- modulation: float32 [12, 1152], P('groups'), parts along dimension 0, may hold values from -3 to 3
- spatial_input: bfloat16 [1152, 3456], replicated, may hold values from -1 to 1
- spatial_output: bfloat16 [1152, 1152], replicated, may hold values from -0.1875 to 0.1875
- temporal_input: bfloat16 [1152, 3456], replicated, may hold values from -1 to 1
- temporal_output: bfloat16 [1152, 1152], replicated, may hold values from -0.1875 to 0.1875
Outputs:
- refined: bfloat16 [64, 1024, 1152], P(('groups', 'wide')), parts along dimension 0
There are 2 independent parts, one for each index of `groups`. A program takes and returns all parts, laid end to end along the dimension named above; an argument that names none is the same for every part. Nothing has to cross between parts.
All inputs are finite; a program needn't handle non-finite values.
Results may differ from a plain program's by a relative error of at most 0.0052.
Values may be sent and summed in bfloat16 or wider, within the bound.
No kernel may reach another device: no remote copies, remote signals or barrier semaphores. Data moves between devices by JAX's collectives and lax.ppermute only.
A program may use at most 320 MiB of HBM per device.

v0:
```python
import functools
import math

import jax
import jax.numpy as jnp
from jax import lax
from jax.experimental import pallas as pl
from jax.experimental.pallas import tpu as pltpu
from jax.sharding import PartitionSpec as P

HEADS = 16
HEAD_DIM = 72
EPSILON = 1e-06
SCORE_SCALE = math.log2(math.e) / math.sqrt(HEAD_DIM)
LANES = 128
WINDOW = 2 * LANES
FAR = -1e30
VMEM_LIMIT = 63 * 1024 * 1024
BLOCKS = 4
RETURNS = ((0, 1), (2, 3))
HEADS_AT_ONCE = 4


def departures(frames):
    if frames == 2:
        return (((0, 0), (0, 1), (0, 2)), ((1, 0), (1, 1)), ((0, 3), (1, 2), (1, 3)))
    whole = [tuple((frame, block) for frame in range(frames)) for block in range(BLOCKS)]
    return (whole[0], whole[1], whole[2] + whole[3])


def pick(step, values):
    chosen = values[0]
    for index in range(1, len(values)):
        chosen = jnp.where(step == index, values[index], chosen)
    return chosen


def normalize(values, offset_row, stretch):
    average = jnp.mean(values, axis=-1, keepdims=True)
    centered = values - average
    spread = jnp.mean(centered * centered, axis=-1, keepdims=True)
    return (centered * lax.rsqrt(spread + EPSILON) * (1.0 + stretch) + offset_row).astype(
        jnp.bfloat16
    )


def head_window(head, features):
    last = features // LANES - 2
    if isinstance(head, int):
        tile = min(head * HEAD_DIM // LANES, last)
        return tile * LANES, head * HEAD_DIM - tile * LANES
    tile = jnp.minimum(head * HEAD_DIM // LANES, last)
    return pl.multiple_of(tile * LANES, LANES), head * HEAD_DIM - tile * LANES


def attend_head(head, q_of, k_of, v_of, total, rows, features, allowed=None):
    lane, first = head_window(head, features)
    lanes = lax.broadcasted_iota(jnp.int32, (rows.size, WINDOW), 1)
    mine = (lanes >= first) & (lanes < first + HEAD_DIM)
    scores = lax.dot_general(
        jnp.where(mine, q_of(lane), 0),
        k_of(lane),
        (((1,), (1,)), ((), ())),
        preferred_element_type=jnp.float32,
    )
    if allowed is not None:
        scores = jnp.where(allowed, scores, FAR)
    largest = jnp.max(scores, axis=-1, keepdims=True)
    powers = jnp.exp2(scores - largest)
    weight = jnp.sum(powers, axis=-1, keepdims=True)
    mixed = jnp.dot(powers.astype(jnp.bfloat16), v_of(lane), preferred_element_type=jnp.float32)
    mixed = jnp.where(mine, mixed * (1.0 / weight), 0.0)
    total[rows, pl.ds(lane, WINDOW)] = total[rows, pl.ds(lane, WINDOW)] + mixed


def project_space_kernel(x_ref, mod_ref, w_ref, *rest):
    o_ref = rest[-1]
    features = x_ref.shape[1]
    normed = normalize(x_ref[...].astype(jnp.float32), mod_ref[0:1, :], mod_ref[1:2, :])
    product = jnp.dot(normed, w_ref[...], preferred_element_type=jnp.float32)
    o_ref[:, :features] = (product[:, :features] * SCORE_SCALE).astype(jnp.bfloat16)
    o_ref[:, features:] = product[:, features:].astype(jnp.bfloat16)


def project_space(video, frame, modulation, weights, into):
    frames, sites, features = video.shape
    block = 128
    first = frame * (sites // block)
    operands = [video.reshape(-1, features), modulation, weights]
    in_specs = [
        pl.BlockSpec((block, features), lambda r: (first + r, 0)),
        pl.BlockSpec(modulation.shape, lambda r: (0, 0)),
        pl.BlockSpec(weights.shape, lambda r: (0, 0), pipeline_mode=pl.Buffered(1)),
    ]
    aliases = {}
    if into is not None:
        operands.append(into)
        in_specs.append(pl.BlockSpec(memory_space=pl.ANY))
        aliases = {3: 0}
    return pl.pallas_call(
        project_space_kernel,
        out_shape=jax.ShapeDtypeStruct((frames * sites, 3 * features), jnp.bfloat16),
        grid=(sites // block,),
        in_specs=in_specs,
        out_specs=pl.BlockSpec((block, 3 * features), lambda r: (first + r, 0)),
        input_output_aliases=aliases,
        compiler_params=pltpu.CompilerParams(vmem_limit_bytes=VMEM_LIMIT),
        cost_estimate=pl.CostEstimate(
            flops=2 * sites * features * 3 * features,
            bytes_accessed=2 * (4 * sites * features + 3 * features * features),
            transcendentals=0,
        ),
        name="space_project",
    )(*operands)


def attend_space_kernel(x_ref, q_ref, k_ref, v_ref, mod_ref, w_ref, o_ref, total):
    rows, features = q_ref.shape
    total[...] = jnp.zeros_like(total)
    for head in range(HEADS):
        attend_head(
            head,
            lambda lane: q_ref[:, pl.ds(lane, WINDOW)],
            lambda lane: k_ref[:, pl.ds(lane, WINDOW)],
            lambda lane: v_ref[:, pl.ds(lane, WINDOW)],
            total,
            pl.ds(0, rows),
            features,
        )
    branch = jnp.dot(
        total[...].astype(jnp.bfloat16), w_ref[...], preferred_element_type=jnp.float32
    )
    halfway = x_ref[0].astype(jnp.float32) + mod_ref[2:3, :] * branch
    o_ref[...] = halfway.astype(jnp.bfloat16).reshape(o_ref.shape)


def attend_space(video, triples, modulation, weights, group, devices):
    _, sites, features = video.shape
    block = sites // BLOCKS
    per = block // devices
    count = len(group)

    def frame(s):
        return pick(s, [f for f, _ in group])

    def place(s):
        return pick(s, [b for _, b in group])

    return pl.pallas_call(
        attend_space_kernel,
        out_shape=jax.ShapeDtypeStruct((devices, count, per, features), jnp.bfloat16),
        grid=(count,),
        in_specs=[
            pl.BlockSpec((1, block, features), lambda s: (frame(s), place(s), 0)),
            pl.BlockSpec((block, features), lambda s: (frame(s) * BLOCKS + place(s), 0)),
            pl.BlockSpec((sites, features), lambda s: (frame(s), 1)),
            pl.BlockSpec((sites, features), lambda s: (frame(s), 2)),
            pl.BlockSpec(modulation.shape, lambda s: (0, 0)),
            pl.BlockSpec(weights.shape, lambda s: (0, 0)),
        ],
        out_specs=pl.BlockSpec((devices, 1, per, features), lambda s: (0, s, 0, 0)),
        scratch_shapes=[pltpu.VMEM((block, features), jnp.float32)],
        compiler_params=pltpu.CompilerParams(vmem_limit_bytes=VMEM_LIMIT),
        cost_estimate=pl.CostEstimate(
            flops=2 * count * block * (features * features + 2 * sites * HEADS * WINDOW),
            bytes_accessed=2 * features * (3 * count * block + 2 * sites + features),
            transcendentals=count * block * sites * HEADS,
        ),
        name="space_attend",
    )(video, triples, triples, triples, modulation, weights)


def time_kernel(sources, mod_ref, wi_ref, wo_ref, *rest):
    o_ref, stream, triples, total = rest[-4:]
    step = pl.program_id(0)
    devices, frames, per, features = o_ref.shape
    groups = per // 8
    size = devices * frames * 8
    share = devices * 8
    for frame, refs in enumerate(sources):
        arrived = pick(step, [rest[index][:, 0] for index in refs]).astype(jnp.float32)
        for g in range(groups):
            stream[pl.ds(g * size + frame * share, share), :] = arrived[
                :, 8 * g : 8 * g + 8, :
            ].reshape(share, features)
    site_of_query = lax.broadcasted_iota(jnp.int32, (size, size), 0) % 8
    site_of_key = lax.broadcasted_iota(jnp.int32, (size, size), 1) % 8

    def one_group(g, carry):
        here = pl.ds(pl.multiple_of(g * size, size), size)
        normed = normalize(stream[here, :], mod_ref[3:4, :], mod_ref[4:5, :])
        product = jnp.dot(normed, wi_ref[...], preferred_element_type=jnp.float32)
        triples[:, :features] = (product[:, :features] * SCORE_SCALE).astype(jnp.bfloat16)
        triples[:, features:] = product[:, features:].astype(jnp.bfloat16)
        total[...] = jnp.zeros_like(total)

        def one_head(head, carry):
            attend_head(
                head,
                lambda lane: triples[:, pl.ds(lane, WINDOW)],
                lambda lane: triples[:, pl.ds(pl.multiple_of(features + lane, LANES), WINDOW)],
                lambda lane: triples[:, pl.ds(pl.multiple_of(2 * features + lane, LANES), WINDOW)],
                total,
                pl.ds(0, size),
                features,
                site_of_query == site_of_key,
            )
            return carry

        lax.fori_loop(0, HEADS, one_head, 0, unroll=HEADS_AT_ONCE)
        branch = jnp.dot(
            total[...].astype(jnp.bfloat16), wo_ref[...], preferred_element_type=jnp.float32
        )
        stream[here, :] = stream[here, :] + mod_ref[5:6, :] * branch
        return carry

    lax.fori_loop(0, groups, one_group, 0)
    for frame in range(frames):
        o_ref[:, frame] = jnp.concatenate(
            [
                stream[pl.ds(g * size + frame * share, share), :].reshape(devices, 8, features)
                for g in range(groups)
            ],
            axis=1,
        ).astype(jnp.bfloat16)


def attend_time(arrived, blocks, frames, modulation, wide_weights, weights):
    operands = [modulation, wide_weights, weights]
    in_specs = [
        pl.BlockSpec(modulation.shape, lambda s: (0, 0)),
        pl.BlockSpec(wide_weights.shape, lambda s: (0, 0), pipeline_mode=pl.Buffered(1)),
        pl.BlockSpec(weights.shape, lambda s: (0, 0), pipeline_mode=pl.Buffered(1)),
    ]
    sources = []
    for frame in range(frames):
        arrays, slots, refs = [], [], []
        for block in blocks:
            array, slot = arrived[frame, block]
            known = [index for index, other in enumerate(arrays) if other is array]
            if not known:
                known = [len(arrays)]
                arrays.append(array)
                slots.append([])
            slots[known[0]].append(slot)
            refs.append(len(operands) - 3 + known[0])
        for array, places in zip(arrays, slots):
            devices, _, per, features = array.shape
            in_specs.append(
                pl.BlockSpec(
                    (devices, 1, per, features),
                    lambda s, places=places: (
                        0,
                        pick(s, places) if len(places) > 1 else places[0],
                        0,
                        0,
                    ),
                )
            )
            operands.append(array)
        sources.append(refs if len(arrays) > 1 else refs[:1])
    rows = devices * frames * per
    size = devices * frames * 8
    return pl.pallas_call(
        functools.partial(time_kernel, sources),
        out_shape=jax.ShapeDtypeStruct(
            (devices, frames, len(blocks) * per, features), jnp.bfloat16
        ),
        grid=(len(blocks),),
        in_specs=in_specs,
        out_specs=pl.BlockSpec((devices, frames, per, features), lambda s: (0, 0, s, 0)),
        scratch_shapes=[
            pltpu.VMEM((rows, features), jnp.float32),
            pltpu.VMEM((size, 3 * features), jnp.bfloat16),
            pltpu.VMEM((size, features), jnp.float32),
        ],
        compiler_params=pltpu.CompilerParams(vmem_limit_bytes=VMEM_LIMIT),
        cost_estimate=pl.CostEstimate(
            flops=len(blocks)
            * (
                2 * rows * features * 4 * features
                + 4 * rows * 8 * devices * frames * HEADS * WINDOW
            ),
            bytes_accessed=len(blocks) * 4 * rows * features + 8 * features * features,
            transcendentals=len(blocks) * rows * 8 * devices * frames * HEADS,
        ),
        name="time_block",
    )(*operands)


def place_sites(piece, into, first, count):
    owners, frames, sites, features = piece.shape
    per = sites // count
    stage = owners // 4

    def place_kernel(x_hbm, *rest):
        o_hbm, held, arriving, leaving = rest[-4:]
        inward = [
            pltpu.make_async_copy(
                x_hbm.at[pl.ds(low, stage)], held.at[pl.ds(low, stage)], arriving.at[index]
            )
            for index, low in enumerate(range(0, owners, stage))
        ]
        for copy in inward:
            copy.start()
        outward = []
        for index, low in enumerate(range(0, owners, stage)):
            inward[index].wait()
            for frame in range(frames):
                for block in range(count):
                    outward.append(
                        pltpu.make_async_copy(
                            held.at[pl.ds(low, stage), frame, pl.ds(block * per, per)],
                            o_hbm.at[frame, pl.ds((first + block) * owners + low, stage)],
                            leaving.at[len(outward)],
                        )
                    )
                    outward[-1].start()
        for copy in outward:
            copy.wait()

    operands = [piece]
    aliases = {}
    if into is not None:
        operands.append(into)
        aliases = {1: 0}
    return pl.pallas_call(
        place_kernel,
        out_shape=jax.ShapeDtypeStruct((frames, BLOCKS * owners, per, features), jnp.bfloat16),
        in_specs=[pl.BlockSpec(memory_space=pl.ANY)] * len(operands),
        out_specs=pl.BlockSpec(memory_space=pl.ANY),
        scratch_shapes=[
            pltpu.VMEM(piece.shape, jnp.bfloat16),
            pltpu.SemaphoreType.DMA((4,)),
            pltpu.SemaphoreType.DMA((4 * frames * count,)),
        ],
        input_output_aliases=aliases,
        compiler_params=pltpu.CompilerParams(vmem_limit_bytes=VMEM_LIMIT),
        cost_estimate=pl.CostEstimate(
            flops=0, bytes_accessed=4 * piece.size, transcendentals=0
        ),
        name="place_sites",
    )(*operands)


def exchange(pieces, earlier):
    if earlier is not None:
        pieces, earlier = lax.optimization_barrier((pieces, earlier))
    return lax.all_to_all(pieces, "wide", split_axis=0, concat_axis=0, tiled=True), earlier


def on_device(video, modulation, spatial_input, spatial_output, temporal_input, temporal_output):
    frames, sites, features = video.shape
    devices = lax.axis_size("wide")
    triples = None
    projected = set()
    landings = []
    arrived = {}
    landed = None
    for group in departures(frames):
        for frame in sorted({frame for frame, _ in group} - projected):
            triples = project_space(video, frame, modulation, spatial_input, triples)
            projected.add(frame)
        leaving = attend_space(video, triples, modulation, spatial_output, group, devices)
        leaving, triples = lax.optimization_barrier((leaving, triples))
        landed, earlier = exchange(leaving, landed)
        landings[-1:] = [earlier, landed] if landings else [landed]
        for slot, pair in enumerate(group):
            arrived[pair] = len(landings) - 1, slot
    refined = None
    for blocks in RETURNS:
        done = attend_time(
            {pair: (landings[index], slot) for pair, (index, slot) in arrived.items()},
            blocks,
            frames,
            modulation,
            temporal_input,
            temporal_output,
        )
        last = landed is landings[-1]
        landed, earlier = exchange(done, landed)
        if last:
            landings[-1] = earlier
        else:
            back = earlier
            refined = place_sites(back, refined, previous[0], len(previous))
        previous = blocks
    refined = place_sites(landed, refined, previous[0], len(previous))
    return refined.reshape(video.shape)


def solution(mesh):
    placed = (P(("groups", "wide"), None, None), P("groups", None), P(), P(), P(), P())
    return jax.shard_map(
        on_device,
        mesh=mesh,
        in_specs=placed,
        out_specs=P(("groups", "wide"), None, None),
        check_vma=False,
    )
```

profile of v0, /device:TPU:13, one launch (start us, length us, event | category | flops | bytes accessed | tf_op | source)
XLA Modules:
  0.0 284.2 jit_solution(1859482150209565105)
XLA Ops:
  0.0 17.0 %space_project.2.q_ref.k_ref.v_ref.rest_0_ = bf16[2048,3456]{1,0:T(8,128)(2,1)} custom-call(bf16[2048,1152]{1,0:T(8,128)(2,1)} %bitcast.2, f32[6,1152]{1,0:T(8,128)} %mod_ref.13, bf16[1152,3456]{1,0:T(8,128)(2,1)} %w_ref.7), custom_call_target="tpu_custom_call" | custom-call | flops 8153726976 | bytes 17399808 | tf_op jit(solution)/shard_map/space_project/pallas_call | solution.py:100
  17.0 23.1 %space_attend.3 = bf16[16,3,16,1152]{3,2,1,0:T(8,128)(2,1)} custom-call(bf16[2,1024,1152]{2,1,0:T(8,128)(2,1)} %x_ref.5, bf16[2048,3456]{1,0:T(8,128)(2,1)} %space_project.2.q_ref.k_ref.v_ref.rest_0_, bf16[2048,3456]{1,0:T(8,128)(2,1)} %space_project.2.q_ref.k_ref.v_ref.rest_0_, bf16[2048,3456]{1,0:T(8,128)(2,1)} %space_project.2.q_ref.k_ref.v_ref.rest_0_, ...), custom_call_target="tpu_custom_call" | custom-call | flops 14923333632 | bytes 12681216 | tf_op jit(solution)/shard_map/space_attend/pallas_call | solution.py:149
  40.1 6.6 %all-to-all-start = ((bf16[16,3,16,1152]{3,2,1,0:T(8,128)(2,1)}), bf16[16,3,16,1152]{3,2,1,0:T(8,128)(2,1)}, u32[]{:S(2)}, u32[]{:S(2)}) async-start(bf16[16,3,16,1152]{3,2,1,0:T(8,128)(2,1)} %space_attend.3), calls=%async_computation | async-start | bytes 3538944 | tf_op jit(solution)/shard_map/all_to_all | solution.py:349
  46.7 17.0 %space_project.3.q_ref.k_ref.v_ref = bf16[2048,3456]{1,0:T(8,128)(2,1)} custom-call(bf16[2048,1152]{1,0:T(8,128)(2,1)} %bitcast.3, f32[6,1152]{1,0:T(8,128)} %mod_ref.13, bf16[1152,3456]{1,0:T(8,128)(2,1)} %w_ref.7, bf16[2048,3456]{1,0:T(8,128)(2,1)} %space_project.2.q_ref.k_ref.v_ref.rest_0_), custom_call_target="tpu_custom_call", output_to_operand_aliasing={{}: (3, {})} | custom-call | flops 8153726976 | bytes 17399808 | tf_op jit(solution)/shard_map/space_project/pallas_call | solution.py:100
  63.6 16.9 %space_attend.4 = bf16[16,2,16,1152]{3,2,1,0:T(8,128)(2,1)} custom-call(bf16[2,1024,1152]{2,1,0:T(8,128)(2,1)} %x_ref.5, bf16[2048,3456]{1,0:T(8,128)(2,1)} %space_project.3.q_ref.k_ref.v_ref, bf16[2048,3456]{1,0:T(8,128)(2,1)} %space_project.3.q_ref.k_ref.v_ref, bf16[2048,3456]{1,0:T(8,128)(2,1)} %space_project.3.q_ref.k_ref.v_ref, f32[6,1152]{1,0:T(8,128)} %mod_ref.13, ...), custom_call_target="tpu_custom_call" | custom-call | flops 9948889088 | bytes 10911744 | tf_op jit(solution)/shard_map/space_attend/pallas_call | solution.py:149
  80.5 6.6 %all-to-all-done.rest_0_ = bf16[16,3,16,1152]{3,2,1,0:T(8,128)(2,1)} async-done(((bf16[16,3,16,1152]{3,2,1,0:T(8,128)(2,1)}), bf16[16,3,16,1152]{3,2,1,0:T(8,128)(2,1)}, u32[]{:S(2)}, u32[]{:S(2)}) %all-to-all-start) | async-done | bytes 1769504 | tf_op jit(solution)/shard_map/all_to_all | solution.py:349
  87.2 4.9 %all-to-all-start.1 = ((bf16[16,2,16,1152]{3,2,1,0:T(8,128)(2,1)}), bf16[16,2,16,1152]{3,2,1,0:T(8,128)(2,1)}, u32[]{:S(2)}, u32[]{:S(2)}) async-start(bf16[16,2,16,1152]{3,2,1,0:T(8,128)(2,1)} %space_attend.4), calls=%async_computation.1 | async-start | bytes 2359296 | tf_op jit(solution)/shard_map/all_to_all | solution.py:349
  92.1 23.4 %space_attend.5 = bf16[16,3,16,1152]{3,2,1,0:T(8,128)(2,1)} custom-call(bf16[2,1024,1152]{2,1,0:T(8,128)(2,1)} %x_ref.5, bf16[2048,3456]{1,0:T(8,128)(2,1)} %space_project.3.q_ref.k_ref.v_ref, bf16[2048,3456]{1,0:T(8,128)(2,1)} %space_project.3.q_ref.k_ref.v_ref, bf16[2048,3456]{1,0:T(8,128)(2,1)} %space_project.3.q_ref.k_ref.v_ref, f32[6,1152]{1,0:T(8,128)} %mod_ref.13, ...), custom_call_target="tpu_custom_call" | custom-call | flops 14923333632 | bytes 12681216 | tf_op jit(solution)/shard_map/space_attend/pallas_call | solution.py:149
  115.4 4.5 %all-to-all-done.1.rest_1_ = bf16[16,2,16,1152]{3,2,1,0:T(8,128)(2,1)} async-done(((bf16[16,2,16,1152]{3,2,1,0:T(8,128)(2,1)}), bf16[16,2,16,1152]{3,2,1,0:T(8,128)(2,1)}, u32[]{:S(2)}, u32[]{:S(2)}) %all-to-all-start.1) | async-done | bytes 1179680 | tf_op jit(solution)/shard_map/all_to_all | solution.py:349
  119.9 4.9 %all-to-all-start.2 = ((bf16[16,3,16,1152]{3,2,1,0:T(8,128)(2,1)}), bf16[16,3,16,1152]{3,2,1,0:T(8,128)(2,1)}, u32[]{:S(2)}, u32[]{:S(2)}) async-start(bf16[16,3,16,1152]{3,2,1,0:T(8,128)(2,1)} %space_attend.5), calls=%async_computation.2 | async-start | bytes 3538944 | tf_op jit(solution)/shard_map/all_to_all | solution.py:349
  124.8 35.6 %time_block.2 = bf16[16,2,32,1152]{3,2,1,0:T(8,128)(2,1)} custom-call(f32[6,1152]{1,0:T(8,128)} %mod_ref.13, bf16[1152,3456]{1,0:T(8,128)(2,1)} %wi_ref.3, bf16[1152,1152]{1,0:T(8,128)(2,1)} %wo_ref.3, bf16[16,3,16,1152]{3,2,1,0:T(8,128)(2,1)} %all-to-all-done.rest_0_, bf16[16,2,16,1152]{3,2,1,0:T(8,128)(2,1)} %all-to-all-done.1.rest_1_), custom_call_target="tpu_custom_call" | custom-call | flops 15166603264 | bytes 15335424 | tf_op jit(solution)/shard_map/time_block/pallas_call | solution.py:264
  160.4 4.9 %all-to-all-done.2.rest_1_.rest_2_ = bf16[16,3,16,1152]{3,2,1,0:T(8,128)(2,1)} async-done(((bf16[16,3,16,1152]{3,2,1,0:T(8,128)(2,1)}), bf16[16,3,16,1152]{3,2,1,0:T(8,128)(2,1)}, u32[]{:S(2)}, u32[]{:S(2)}) %all-to-all-start.2) | async-done | bytes 1769504 | tf_op jit(solution)/shard_map/all_to_all | solution.py:349
  165.3 4.9 %all-to-all-start.3 = ((bf16[16,2,32,1152]{3,2,1,0:T(8,128)(2,1)}), bf16[16,2,32,1152]{3,2,1,0:T(8,128)(2,1)}, u32[]{:S(2)}, u32[]{:S(2)}) async-start(bf16[16,2,32,1152]{3,2,1,0:T(8,128)(2,1)} %time_block.2), calls=%async_computation.3 | async-start | bytes 4718592 | tf_op jit(solution)/shard_map/all_to_all | solution.py:349
  170.2 35.7 %time_block.3 = bf16[16,2,32,1152]{3,2,1,0:T(8,128)(2,1)} custom-call(f32[6,1152]{1,0:T(8,128)} %mod_ref.13, bf16[1152,3456]{1,0:T(8,128)(2,1)} %wi_ref.3, bf16[1152,1152]{1,0:T(8,128)(2,1)} %wo_ref.3, bf16[16,3,16,1152]{3,2,1,0:T(8,128)(2,1)} %all-to-all-done.rest_0_, bf16[16,3,16,1152]{3,2,1,0:T(8,128)(2,1)} %all-to-all-done.2.rest_1_.rest_2_, ...), custom_call_target="tpu_custom_call" | custom-call | flops 15166603264 | bytes 15335424 | tf_op jit(solution)/shard_map/time_block/pallas_call | solution.py:264
  205.9 17.4 %all-to-all-done.3.x_hbm = bf16[16,2,32,1152]{3,2,1,0:T(8,128)(2,1)} async-done(((bf16[16,2,32,1152]{3,2,1,0:T(8,128)(2,1)}), bf16[16,2,32,1152]{3,2,1,0:T(8,128)(2,1)}, u32[]{:S(2)}, u32[]{:S(2)}) %all-to-all-start.3) | async-done | bytes 2359328 | tf_op jit(solution)/shard_map/all_to_all | solution.py:349
  223.4 4.9 %all-to-all-start.4 = ((bf16[16,2,32,1152]{3,2,1,0:T(8,128)(2,1)}), bf16[16,2,32,1152]{3,2,1,0:T(8,128)(2,1)}, u32[]{:S(2)}, u32[]{:S(2)}) async-start(bf16[16,2,32,1152]{3,2,1,0:T(8,128)(2,1)} %time_block.3), calls=%async_computation.4 | async-start | bytes 4718592 | tf_op jit(solution)/shard_map/all_to_all | solution.py:349
  228.3 2.6 place_sites.2.rest_0_
  230.9 50.5 %all-to-all-done.4.x_hbm = bf16[16,2,32,1152]{3,2,1,0:T(8,128)(2,1)} async-done(((bf16[16,2,32,1152]{3,2,1,0:T(8,128)(2,1)}), bf16[16,2,32,1152]{3,2,1,0:T(8,128)(2,1)}, u32[]{:S(2)}, u32[]{:S(2)}) %all-to-all-start.4) | async-done | bytes 2359328 | tf_op jit(solution)/shard_map/all_to_all | solution.py:349
  281.4 2.6 place_sites.3
Async XLA Ops:
  40.1 47.1 %all-to-all-start = ((bf16[16,3,16,1152]{3,2,1,0:T(8,128)(2,1)}), bf16[16,3,16,1152]{3,2,1,0:T(8,128)(2,1)}, u32[]{:S(2)}, u32[]{:S(2)}) async-start(bf16[16,3,16,1152]{3,2,1,0:T(8,128)(2,1)} %space_attend.3), calls=%async_computation | async-start | bytes 3538944 | tf_op jit(solution)/shard_map/all_to_all | solution.py:349
  87.2 32.8 %all-to-all-start.1 = ((bf16[16,2,16,1152]{3,2,1,0:T(8,128)(2,1)}), bf16[16,2,16,1152]{3,2,1,0:T(8,128)(2,1)}, u32[]{:S(2)}, u32[]{:S(2)}) async-start(bf16[16,2,16,1152]{3,2,1,0:T(8,128)(2,1)} %space_attend.4), calls=%async_computation.1 | async-start | bytes 2359296 | tf_op jit(solution)/shard_map/all_to_all | solution.py:349
  119.9 45.4 %all-to-all-start.2 = ((bf16[16,3,16,1152]{3,2,1,0:T(8,128)(2,1)}), bf16[16,3,16,1152]{3,2,1,0:T(8,128)(2,1)}, u32[]{:S(2)}, u32[]{:S(2)}) async-start(bf16[16,3,16,1152]{3,2,1,0:T(8,128)(2,1)} %space_attend.5), calls=%async_computation.2 | async-start | bytes 3538944 | tf_op jit(solution)/shard_map/all_to_all | solution.py:349
  165.3 58.1 %all-to-all-start.3 = ((bf16[16,2,32,1152]{3,2,1,0:T(8,128)(2,1)}), bf16[16,2,32,1152]{3,2,1,0:T(8,128)(2,1)}, u32[]{:S(2)}, u32[]{:S(2)}) async-start(bf16[16,2,32,1152]{3,2,1,0:T(8,128)(2,1)} %time_block.2), calls=%async_computation.3 | async-start | bytes 4718592 | tf_op jit(solution)/shard_map/all_to_all | solution.py:349
  223.4 58.1 %all-to-all-start.4 = ((bf16[16,2,32,1152]{3,2,1,0:T(8,128)(2,1)}), bf16[16,2,32,1152]{3,2,1,0:T(8,128)(2,1)}, u32[]{:S(2)}, u32[]{:S(2)}) async-start(bf16[16,2,32,1152]{3,2,1,0:T(8,128)(2,1)} %time_block.3), calls=%async_computation.4 | async-start | bytes 4718592 | tf_op jit(solution)/shard_map/all_to_all | solution.py:349
where the time goes:
time: 285 us; the launch traced here: 284 us
  Pallas kernels  174 us (61%)
  waiting for transfers between devices  84 us (29%)
  starting transfers between devices  26.2 us (9%)
    all_to_all x5, waiting for transfers between devices, exchange(): lax.all_to_all(pieces, 'wide', split_axis=0, concat_axis=0, tiled=True)  84 us
    pallas_call x2, Pallas kernels, attend_time(): pl.pallas_call(functools.partial(time_kernel, sources), out_shape=jax.Sha...  71.3 us
    pallas_call x3, Pallas kernels, attend_space(): pl.pallas_call(attend_space_kernel, out_shape=jax.ShapeDtypeStruct((devic...  63.4 us
    pallas_call x2, Pallas kernels, project_space(): pl.pallas_call(project_space_kernel, out_shape=jax.ShapeDtypeStruct((fram...  33.9 us
    all_to_all x5, starting transfers between devices, exchange(): lax.all_to_all(pieces, 'wide', split_axis=0, concat_axis=0, tiled=True)  26.2 us
  transfers between devices with their start and end apart: 5, of which 5 were waited for; matrix products, arithmetic and copies ran while one was open for 0% of the time, Pallas kernels for 46%

commit v1 on v0

--- a/solution.py
+++ b/solution.py
@@ -23,7 +23,7 @@
 
 def departures(frames):
     if frames == 2:
-        return (((0, 0), (0, 1), (0, 2)), ((1, 0), (1, 1)), ((0, 3), (1, 2), (1, 3)))
+        return (((0, 0), (0, 1)), ((1, 0), (1, 1)), ((0, 2), (0, 3), (1, 2), (1, 3)))
     whole = [tuple((frame, block) for frame in range(frames)) for block in range(BLOCKS)]
     return (whole[0], whole[1], whole[2] + whole[3])
 
@@ -73,65 +73,131 @@
     total[rows, pl.ds(lane, WINDOW)] = total[rows, pl.ds(lane, WINDOW)] + mixed
 
 
-def project_space_kernel(x_ref, mod_ref, w_ref, *rest):
-    o_ref = rest[-1]
-    features = x_ref.shape[1]
-    normed = normalize(x_ref[...].astype(jnp.float32), mod_ref[0:1, :], mod_ref[1:2, :])
+def attend_heads(q_of, k_of, v_of, total, x_ref, mod_ref, w_ref, o_ref):
+    rows, features = total.shape
+    total[...] = jnp.zeros_like(total)
+    for head in range(HEADS):
+        attend_head(head, q_of, k_of, v_of, total, pl.ds(0, rows), features)
+    branch = jnp.dot(
+        total[...].astype(jnp.bfloat16), w_ref[...], preferred_element_type=jnp.float32
+    )
+    halfway = x_ref[0].astype(jnp.float32) + mod_ref[2:3, :] * branch
+    o_ref[...] = halfway.astype(jnp.bfloat16).reshape(o_ref.shape)
+
+
+def project(values, mod_ref, row, w_ref, target, rows):
+    features = values.shape[1]
+    normed = normalize(values, mod_ref[row : row + 1, :], mod_ref[row + 1 : row + 2, :])
     product = jnp.dot(normed, w_ref[...], preferred_element_type=jnp.float32)
-    o_ref[:, :features] = (product[:, :features] * SCORE_SCALE).astype(jnp.bfloat16)
-    o_ref[:, features:] = product[:, features:].astype(jnp.bfloat16)
-
-
-def project_space(video, frame, modulation, weights, into):
+    target[rows, :features] = (product[:, :features] * SCORE_SCALE).astype(jnp.bfloat16)
+    target[rows, features:] = product[:, features:].astype(jnp.bfloat16)
+
+
+def open_space_kernel(frame, blocks, x_ref, mod_ref, wi_ref, wo_hbm, *rest):
+    o_ref, t_hbm, triples, total, wo_ref, semaphores = rest[-6:]
+    step = pl.program_id(0)
+    _, rows, features = x_ref.shape
+    sites = triples.shape[0]
+    count = sites // rows
+
+    def keep(block):
+        here = pl.ds(pl.multiple_of(block * rows, rows), rows)
+        there = pl.ds(pl.multiple_of(frame * sites + block * rows, rows), rows)
+        return pltpu.make_async_copy(triples.at[here], t_hbm.at[there], semaphores.at[block])
+
+    fetch = pltpu.make_async_copy(wo_hbm, wo_ref, semaphores.at[count])
+    pl.when(step == 0)(fetch.start)
+    pl.when(step == count)(fetch.wait)
+
+    @pl.when(step < count)
+    def _():
+        here = pl.ds(pl.multiple_of(step * rows, rows), rows)
+        project(x_ref[0].astype(jnp.float32), mod_ref, 0, wi_ref, triples, here)
+        keep(step).start()
+
+    @pl.when(step >= count)
+    def _():
+        first = pl.multiple_of(pick(step - count, blocks) * rows, rows)
+        attend_heads(
+            lambda lane: triples[pl.ds(first, rows), pl.ds(lane, WINDOW)],
+            lambda lane: triples[:, pl.ds(features + lane, WINDOW)],
+            lambda lane: triples[:, pl.ds(2 * features + lane, WINDOW)],
+            total,
+            x_ref,
+            mod_ref,
+            wo_ref,
+            o_ref,
+        )
+
+    @pl.when(step == count + len(blocks) - 1)
+    def _():
+        for block in range(count):
+            keep(block).wait()
+
+
+def open_space(video, modulation, wide_weights, weights, frame, blocks, into, devices):
     frames, sites, features = video.shape
-    block = 128
-    first = frame * (sites // block)
-    operands = [video.reshape(-1, features), modulation, weights]
+    block = sites // BLOCKS
+    per = block // devices
+    operands = [video, modulation, wide_weights, weights]
     in_specs = [
-        pl.BlockSpec((block, features), lambda r: (first + r, 0)),
-        pl.BlockSpec(modulation.shape, lambda r: (0, 0)),
-        pl.BlockSpec(weights.shape, lambda r: (0, 0), pipeline_mode=pl.Buffered(1)),
+        pl.BlockSpec(
+            (1, block, features),
+            lambda s: (frame, jnp.where(s < BLOCKS, s, pick(s - BLOCKS, blocks)), 0),
+        ),
+        pl.BlockSpec(modulation.shape, lambda s: (0, 0)),
+        pl.BlockSpec(wide_weights.shape, lambda s: (0, 0), pipeline_mode=pl.Buffered(1)),
+        pl.BlockSpec(memory_space=pl.ANY),
     ]
     aliases = {}
     if into is not None:
         operands.append(into)
         in_specs.append(pl.BlockSpec(memory_space=pl.ANY))
-        aliases = {3: 0}
+        aliases = {4: 1}
+    count = len(blocks)
     return pl.pallas_call(
-        project_space_kernel,
-        out_shape=jax.ShapeDtypeStruct((frames * sites, 3 * features), jnp.bfloat16),
-        grid=(sites // block,),
+        functools.partial(open_space_kernel, frame, blocks),
+        out_shape=[
+            jax.ShapeDtypeStruct((devices, count, per, features), jnp.bfloat16),
+            jax.ShapeDtypeStruct((frames * sites, 3 * features), jnp.bfloat16),
+        ],
+        grid=(BLOCKS + count,),
         in_specs=in_specs,
-        out_specs=pl.BlockSpec((block, 3 * features), lambda r: (first + r, 0)),
+        out_specs=[
+            pl.BlockSpec(
+                (devices, 1, per, features), lambda s: (0, jnp.maximum(s - BLOCKS, 0), 0, 0)
+            ),
+            pl.BlockSpec(memory_space=pl.ANY),
+        ],
+        scratch_shapes=[
+            pltpu.VMEM((sites, 3 * features), jnp.bfloat16),
+            pltpu.VMEM((block, features), jnp.float32),
+            pltpu.VMEM(weights.shape, jnp.bfloat16),
+            pltpu.SemaphoreType.DMA((BLOCKS + 1,)),
+        ],
         input_output_aliases=aliases,
         compiler_params=pltpu.CompilerParams(vmem_limit_bytes=VMEM_LIMIT),
         cost_estimate=pl.CostEstimate(
-            flops=2 * sites * features * 3 * features,
-            bytes_accessed=2 * (4 * sites * features + 3 * features * features),
-            transcendentals=0,
-        ),
-        name="space_project",
+            flops=2 * sites * features * 3 * features
+            + 2 * count * block * (features * features + 2 * sites * HEADS * WINDOW),
+            bytes_accessed=2 * features * (4 * sites + 2 * count * block + 4 * features),
+            transcendentals=count * block * sites * HEADS,
+        ),
+        name="space_open",
     )(*operands)
 
 
 def attend_space_kernel(x_ref, q_ref, k_ref, v_ref, mod_ref, w_ref, o_ref, total):
-    rows, features = q_ref.shape
-    total[...] = jnp.zeros_like(total)
-    for head in range(HEADS):
-        attend_head(
-            head,
-            lambda lane: q_ref[:, pl.ds(lane, WINDOW)],
-            lambda lane: k_ref[:, pl.ds(lane, WINDOW)],
-            lambda lane: v_ref[:, pl.ds(lane, WINDOW)],
-            total,
-            pl.ds(0, rows),
-            features,
-        )
-    branch = jnp.dot(
-        total[...].astype(jnp.bfloat16), w_ref[...], preferred_element_type=jnp.float32
+    attend_heads(
+        lambda lane: q_ref[:, pl.ds(lane, WINDOW)],
+        lambda lane: k_ref[:, pl.ds(lane, WINDOW)],
+        lambda lane: v_ref[:, pl.ds(lane, WINDOW)],
+        total,
+        x_ref,
+        mod_ref,
+        w_ref,
+        o_ref,
     )
-    halfway = x_ref[0].astype(jnp.float32) + mod_ref[2:3, :] * branch
-    o_ref[...] = halfway.astype(jnp.bfloat16).reshape(o_ref.shape)
 
 
 def attend_space(video, triples, modulation, weights, group, devices):
@@ -188,10 +254,15 @@
 
     def one_group(g, carry):
         here = pl.ds(pl.multiple_of(g * size, size), size)
-        normed = normalize(stream[here, :], mod_ref[3:4, :], mod_ref[4:5, :])
-        product = jnp.dot(normed, wi_ref[...], preferred_element_type=jnp.float32)
-        triples[:, :features] = (product[:, :features] * SCORE_SCALE).astype(jnp.bfloat16)
-        triples[:, features:] = product[:, features:].astype(jnp.bfloat16)
+        half = size // 2
+
+        def one_half(h, carry):
+            start = pl.multiple_of(h * half, half)
+            values = stream[pl.ds(pl.multiple_of(g * size + start, half), half), :]
+            project(values, mod_ref, 3, wi_ref, triples, pl.ds(start, half))
+            return carry
+
+        lax.fori_loop(0, 2, one_half, 0)
         total[...] = jnp.zeros_like(total)
 
         def one_head(head, carry):
@@ -353,15 +424,26 @@
     frames, sites, features = video.shape
     devices = lax.axis_size("wide")
     triples = None
-    projected = set()
+    opened = set()
     landings = []
     arrived = {}
     landed = None
     for group in departures(frames):
-        for frame in sorted({frame for frame, _ in group} - projected):
-            triples = project_space(video, frame, modulation, spatial_input, triples)
-            projected.add(frame)
-        leaving = attend_space(video, triples, modulation, spatial_output, group, devices)
+        fresh = sorted({frame for frame, _ in group} - opened)
+        if len(fresh) == 1 and {frame for frame, _ in group} == set(fresh):
+            leaving, triples = open_space(
+                video,
+                modulation,
+                spatial_input,
+                spatial_output,
+                fresh[0],
+                [block for _, block in group],
+                triples,
+                devices,
+            )
+            opened.update(fresh)
+        else:
+            leaving = attend_space(video, triples, modulation, spatial_output, group, devices)
         leaving, triples = lax.optimization_barrier((leaving, triples))
         landed, earlier = exchange(leaving, landed)
         landings[-1:] = [earlier, landed] if landings else [landed]

time: 285 us -> 277 us (0.972)
  Pallas kernels: 174 us -> 166 us
    pallas_call x3 -> x1, Pallas kernels: 63.4 us -> 29.7 us  [attend_space(): pl.pallas_call(attend_space_kernel, out_shape=jax.ShapeDtypeStruct((devic...]
    pallas_call x2, Pallas kernels: 33.9 us -> 56.6 us  [open_space(): pl.pallas_call(functools.partial(open_space_kernel, frame, blocks), out_s...]
  transfers between devices with their start and end apart: 5 -> 5, of which waited for: 5 -> 3; matrix products, arithmetic and copies ran while one was open for 0% -> 0% of each run, Pallas kernels for 46% -> 49%
where the time goes in v1:
time: 277 us
  Pallas kernels  166 us (60%)
  waiting for transfers between devices  82.7 us (30%)
  starting transfers between devices  28.4 us (10%)
    all_to_all x5, waiting for transfers between devices, exchange(): lax.all_to_all(pieces, 'wide', split_axis=0, concat_axis=0, tiled=True)  82.7 us
    pallas_call x2, Pallas kernels, attend_time(): pl.pallas_call(functools.partial(time_kernel, sources), out_shape=jax.Sha...  74.1 us
    pallas_call x2, Pallas kernels, open_space(): pl.pallas_call(functools.partial(open_space_kernel, frame, blocks), out_s...  56.6 us
    pallas_call x1, Pallas kernels, attend_space(): pl.pallas_call(attend_space_kernel, out_shape=jax.ShapeDtypeStruct((devic...  29.7 us
    all_to_all x5, starting transfers between devices, exchange(): lax.all_to_all(pieces, 'wide', split_axis=0, concat_axis=0, tiled=True)  28.4 us
  transfers between devices with their start and end apart: 5, of which 3 were waited for; matrix products, arithmetic and copies ran while one was open for 0% of the time, Pallas kernels for 49%

profile of v1, /device:TPU:13, one launch (start us, length us, event | category | flops | bytes accessed | tf_op | source)
XLA Modules:
  0.0 277.0 jit_solution(14634686115198886561)
XLA Ops:
  0.0 28.3 %space_open.2 = (bf16[16,2,16,1152]{3,2,1,0:T(8,128)(2,1)}, bf16[2048,3456]{1,0:T(8,128)(2,1)}) custom-call(bf16[2,1024,1152]{2,1,0:T(8,128)(2,1)} %x_ref.5, f32[6,1152]{1,0:T(8,128)} %mod_ref.9, bf16[1152,3456]{1,0:T(8,128)(2,1)} %wi_ref.5, bf16[1152,1152]{1,0:T(8,128)(2,1)} %w_ref.1), custom_call_target="tpu_custom_call" | custom-call | flops 18102616064 | bytes 22413312 | tf_op jit(solution)/shard_map/space_open/pallas_call | solution.py:158
  28.3 6.6 %all-to-all-start = ((bf16[16,2,16,1152]{3,2,1,0:T(8,128)(2,1)}), bf16[16,2,16,1152]{3,2,1,0:T(8,128)(2,1)}, u32[]{:S(2)}, u32[]{:S(2)}) async-start(bf16[16,2,16,1152]{3,2,1,0:T(8,128)(2,1)} %get-tuple-element.20), calls=%async_computation | async-start | bytes 2359296 | tf_op jit(solution)/shard_map/all_to_all | solution.py:420
  34.8 28.3 %space_open.3 = (bf16[16,2,16,1152]{3,2,1,0:T(8,128)(2,1)}, bf16[2048,3456]{1,0:T(8,128)(2,1)}) custom-call(bf16[2,1024,1152]{2,1,0:T(8,128)(2,1)} %x_ref.5, f32[6,1152]{1,0:T(8,128)} %mod_ref.9, bf16[1152,3456]{1,0:T(8,128)(2,1)} %wi_ref.5, bf16[1152,1152]{1,0:T(8,128)(2,1)} %w_ref.1, ...), custom_call_target="tpu_custom_call", output_to_operand_aliasing={{1}: (4, {})} | custom-call | flops 18102616064 | bytes 22413312 | tf_op jit(solution)/shard_map/space_open/pallas_call | solution.py:158
  63.2 0.0 all-to-all-done.rest_0_
  63.2 6.0 %all-to-all-start.1 = ((bf16[16,2,16,1152]{3,2,1,0:T(8,128)(2,1)}), bf16[16,2,16,1152]{3,2,1,0:T(8,128)(2,1)}, u32[]{:S(2)}, u32[]{:S(2)}) async-start(bf16[16,2,16,1152]{3,2,1,0:T(8,128)(2,1)} %get-tuple-element.24), calls=%async_computation.1 | async-start | bytes 2359296 | tf_op jit(solution)/shard_map/all_to_all | solution.py:420
  69.2 29.7 %space_attend.1 = bf16[16,4,16,1152]{3,2,1,0:T(8,128)(2,1)} custom-call(bf16[2,1024,1152]{2,1,0:T(8,128)(2,1)} %x_ref.5, bf16[2048,3456]{1,0:T(8,128)(2,1)} %get-tuple-element.22.q_ref.k_ref.v_ref, bf16[2048,3456]{1,0:T(8,128)(2,1)} %get-tuple-element.22.q_ref.k_ref.v_ref, bf16[2048,3456]{1,0:T(8,128)(2,1)} %get-tuple-element.22.q_ref.k_ref.v_ref, ...), custom_call_target="tpu_custom_call" | custom-call | flops 19897778176 | bytes 14450688 | tf_op jit(solution)/shard_map/space_attend/pallas_call | solution.py:215
  98.9 0.0 all-to-all-done.1.rest_1_
  98.9 6.0 %all-to-all-start.2 = ((bf16[16,4,16,1152]{3,2,1,0:T(8,128)(2,1)}), bf16[16,4,16,1152]{3,2,1,0:T(8,128)(2,1)}, u32[]{:S(2)}, u32[]{:S(2)}) async-start(bf16[16,4,16,1152]{3,2,1,0:T(8,128)(2,1)} %space_attend.1), calls=%async_computation.2 | async-start | bytes 4718592 | tf_op jit(solution)/shard_map/all_to_all | solution.py:420
  104.9 37.1 %time_block.2 = bf16[16,2,32,1152]{3,2,1,0:T(8,128)(2,1)} custom-call(f32[6,1152]{1,0:T(8,128)} %mod_ref.9, bf16[1152,3456]{1,0:T(8,128)(2,1)} %wi_ref.7, bf16[1152,1152]{1,0:T(8,128)(2,1)} %wo_ref.3, bf16[16,2,16,1152]{3,2,1,0:T(8,128)(2,1)} %all-to-all-done.rest_0_, bf16[16,2,16,1152]{3,2,1,0:T(8,128)(2,1)} %all-to-all-done.1.rest_1_), custom_call_target="tpu_custom_call" | custom-call | flops 15166603264 | bytes 15335424 | tf_op jit(solution)/shard_map/time_block/pallas_call | solution.py:335
  142.0 16.1 %all-to-all-done.2.rest_0_.rest_1_ = bf16[16,4,16,1152]{3,2,1,0:T(8,128)(2,1)} async-done(((bf16[16,4,16,1152]{3,2,1,0:T(8,128)(2,1)}), bf16[16,4,16,1152]{3,2,1,0:T(8,128)(2,1)}, u32[]{:S(2)}, u32[]{:S(2)}) %all-to-all-start.2) | async-done | bytes 2359328 | tf_op jit(solution)/shard_map/all_to_all | solution.py:420
  158.1 4.9 %all-to-all-start.3 = ((bf16[16,2,32,1152]{3,2,1,0:T(8,128)(2,1)}), bf16[16,2,32,1152]{3,2,1,0:T(8,128)(2,1)}, u32[]{:S(2)}, u32[]{:S(2)}) async-start(bf16[16,2,32,1152]{3,2,1,0:T(8,128)(2,1)} %time_block.2), calls=%async_computation.3 | async-start | bytes 4718592 | tf_op jit(solution)/shard_map/all_to_all | solution.py:420
  163.0 37.0 %time_block.3 = bf16[16,2,32,1152]{3,2,1,0:T(8,128)(2,1)} custom-call(f32[6,1152]{1,0:T(8,128)} %mod_ref.9, bf16[1152,3456]{1,0:T(8,128)(2,1)} %wi_ref.7, bf16[1152,1152]{1,0:T(8,128)(2,1)} %wo_ref.3, bf16[16,4,16,1152]{3,2,1,0:T(8,128)(2,1)} %all-to-all-done.2.rest_0_.rest_1_, bf16[16,4,16,1152]{3,2,1,0:T(8,128)(2,1)} %all-to-all-done.2.rest_0_.rest_1_), custom_call_target="tpu_custom_call" | custom-call | flops 15166603264 | bytes 15335424 | tf_op jit(solution)/shard_map/time_block/pallas_call | solution.py:335
  200.0 16.1 %all-to-all-done.3.x_hbm = bf16[16,2,32,1152]{3,2,1,0:T(8,128)(2,1)} async-done(((bf16[16,2,32,1152]{3,2,1,0:T(8,128)(2,1)}), bf16[16,2,32,1152]{3,2,1,0:T(8,128)(2,1)}, u32[]{:S(2)}, u32[]{:S(2)}) %all-to-all-start.3) | async-done | bytes 2359328 | tf_op jit(solution)/shard_map/all_to_all | solution.py:420
  216.1 4.9 %all-to-all-start.4 = ((bf16[16,2,32,1152]{3,2,1,0:T(8,128)(2,1)}), bf16[16,2,32,1152]{3,2,1,0:T(8,128)(2,1)}, u32[]{:S(2)}, u32[]{:S(2)}) async-start(bf16[16,2,32,1152]{3,2,1,0:T(8,128)(2,1)} %time_block.3), calls=%async_computation.4 | async-start | bytes 4718592 | tf_op jit(solution)/shard_map/all_to_all | solution.py:420
  221.0 2.6 place_sites.2.rest_0_
  223.7 50.5 %all-to-all-done.4.x_hbm = bf16[16,2,32,1152]{3,2,1,0:T(8,128)(2,1)} async-done(((bf16[16,2,32,1152]{3,2,1,0:T(8,128)(2,1)}), bf16[16,2,32,1152]{3,2,1,0:T(8,128)(2,1)}, u32[]{:S(2)}, u32[]{:S(2)}) %all-to-all-start.4) | async-done | bytes 2359328 | tf_op jit(solution)/shard_map/all_to_all | solution.py:420
  274.2 2.6 place_sites.3
Async XLA Ops:
  28.3 34.9 %all-to-all-start = ((bf16[16,2,16,1152]{3,2,1,0:T(8,128)(2,1)}), bf16[16,2,16,1152]{3,2,1,0:T(8,128)(2,1)}, u32[]{:S(2)}, u32[]{:S(2)}) async-start(bf16[16,2,16,1152]{3,2,1,0:T(8,128)(2,1)} %get-tuple-element.20), calls=%async_computation | async-start | bytes 2359296 | tf_op jit(solution)/shard_map/all_to_all | solution.py:420
  63.2 35.7 %all-to-all-start.1 = ((bf16[16,2,16,1152]{3,2,1,0:T(8,128)(2,1)}), bf16[16,2,16,1152]{3,2,1,0:T(8,128)(2,1)}, u32[]{:S(2)}, u32[]{:S(2)}) async-start(bf16[16,2,16,1152]{3,2,1,0:T(8,128)(2,1)} %get-tuple-element.24), calls=%async_computation.1 | async-start | bytes 2359296 | tf_op jit(solution)/shard_map/all_to_all | solution.py:420
  98.9 59.2 %all-to-all-start.2 = ((bf16[16,4,16,1152]{3,2,1,0:T(8,128)(2,1)}), bf16[16,4,16,1152]{3,2,1,0:T(8,128)(2,1)}, u32[]{:S(2)}, u32[]{:S(2)}) async-start(bf16[16,4,16,1152]{3,2,1,0:T(8,128)(2,1)} %space_attend.1), calls=%async_computation.2 | async-start | bytes 4718592 | tf_op jit(solution)/shard_map/all_to_all | solution.py:420
  158.1 58.1 %all-to-all-start.3 = ((bf16[16,2,32,1152]{3,2,1,0:T(8,128)(2,1)}), bf16[16,2,32,1152]{3,2,1,0:T(8,128)(2,1)}, u32[]{:S(2)}, u32[]{:S(2)}) async-start(bf16[16,2,32,1152]{3,2,1,0:T(8,128)(2,1)} %time_block.2), calls=%async_computation.3 | async-start | bytes 4718592 | tf_op jit(solution)/shard_map/all_to_all | solution.py:420
  216.1 58.1 %all-to-all-start.4 = ((bf16[16,2,32,1152]{3,2,1,0:T(8,128)(2,1)}), bf16[16,2,32,1152]{3,2,1,0:T(8,128)(2,1)}, u32[]{:S(2)}, u32[]{:S(2)}) async-start(bf16[16,2,32,1152]{3,2,1,0:T(8,128)(2,1)} %time_block.3), calls=%async_computation.4 | async-start | bytes 4718592 | tf_op jit(solution)/shard_map/all_to_all | solution.py:420

commit v2 on v1

--- a/solution.py
+++ b/solution.py
@@ -16,6 +16,7 @@
 WINDOW = 2 * LANES
 FAR = -1e30
 VMEM_LIMIT = 63 * 1024 * 1024
+PLACE_LIMIT = 16 * 1024 * 1024
 BLOCKS = 4
 RETURNS = ((0, 1), (2, 3))
 HEADS_AT_ONCE = 4
@@ -53,31 +54,42 @@
     return pl.multiple_of(tile * LANES, LANES), head * HEAD_DIM - tile * LANES
 
 
-def attend_head(head, q_of, k_of, v_of, total, rows, features, allowed=None):
+def in_head(rows, first):
+    lanes = lax.broadcasted_iota(jnp.int32, (rows, WINDOW), 1)
+    return (lanes >= first) & (lanes < first + HEAD_DIM)
+
+
+def score_head(head, q_of, k_of, rows, features):
     lane, first = head_window(head, features)
-    lanes = lax.broadcasted_iota(jnp.int32, (rows.size, WINDOW), 1)
-    mine = (lanes >= first) & (lanes < first + HEAD_DIM)
-    scores = lax.dot_general(
-        jnp.where(mine, q_of(lane), 0),
+    return lax.dot_general(
+        jnp.where(in_head(rows, first), q_of(lane), 0),
         k_of(lane),
         (((1,), (1,)), ((), ())),
         preferred_element_type=jnp.float32,
     )
-    if allowed is not None:
-        scores = jnp.where(allowed, scores, FAR)
+
+
+def mix_head(head, scores, v_of, total):
+    rows, features = total.shape
+    lane, first = head_window(head, features)
     largest = jnp.max(scores, axis=-1, keepdims=True)
     powers = jnp.exp2(scores - largest)
     weight = jnp.sum(powers, axis=-1, keepdims=True)
     mixed = jnp.dot(powers.astype(jnp.bfloat16), v_of(lane), preferred_element_type=jnp.float32)
-    mixed = jnp.where(mine, mixed * (1.0 / weight), 0.0)
-    total[rows, pl.ds(lane, WINDOW)] = total[rows, pl.ds(lane, WINDOW)] + mixed
+    mixed = jnp.where(in_head(rows, first), mixed * (1.0 / weight), 0.0)
+    total[:, pl.ds(lane, WINDOW)] = total[:, pl.ds(lane, WINDOW)] + mixed
 
 
 def attend_heads(q_of, k_of, v_of, total, x_ref, mod_ref, w_ref, o_ref):
     rows, features = total.shape
     total[...] = jnp.zeros_like(total)
+    scores = score_head(0, q_of, k_of, rows, features)
     for head in range(HEADS):
-        attend_head(head, q_of, k_of, v_of, total, pl.ds(0, rows), features)
+        following = None
+        if head + 1 < HEADS:
+            following = score_head(head + 1, q_of, k_of, rows, features)
+        mix_head(head, scores, v_of, total)
+        scores = following
     branch = jnp.dot(
         total[...].astype(jnp.bfloat16), w_ref[...], preferred_element_type=jnp.float32
     )
@@ -266,15 +278,18 @@
         total[...] = jnp.zeros_like(total)
 
         def one_head(head, carry):
-            attend_head(
+            scores = score_head(
                 head,
                 lambda lane: triples[:, pl.ds(lane, WINDOW)],
                 lambda lane: triples[:, pl.ds(pl.multiple_of(features + lane, LANES), WINDOW)],
+                size,
+                features,
+            )
+            mix_head(
+                head,
+                jnp.where(site_of_query == site_of_key, scores, FAR),
                 lambda lane: triples[:, pl.ds(pl.multiple_of(2 * features + lane, LANES), WINDOW)],
                 total,
-                pl.ds(0, size),
-                features,
-                site_of_query == site_of_key,
             )
             return carry
 
@@ -362,51 +377,38 @@
 def place_sites(piece, into, first, count):
     owners, frames, sites, features = piece.shape
     per = sites // count
-    stage = owners // 4
-
-    def place_kernel(x_hbm, *rest):
-        o_hbm, held, arriving, leaving = rest[-4:]
-        inward = [
+
+    def place_kernel(x_ref, *rest):
+        o_hbm, semaphores = rest[-2:]
+        copies = [
             pltpu.make_async_copy(
-                x_hbm.at[pl.ds(low, stage)], held.at[pl.ds(low, stage)], arriving.at[index]
+                x_ref.at[:, frame, pl.ds(block * per, per)],
+                o_hbm.at[frame, pl.ds((first + block) * owners, owners)],
+                semaphores.at[frame, block],
             )
-            for index, low in enumerate(range(0, owners, stage))
+            for frame in range(frames)
+            for block in range(count)
         ]
-        for copy in inward:
+        for copy in copies:
             copy.start()
-        outward = []
-        for index, low in enumerate(range(0, owners, stage)):
-            inward[index].wait()
-            for frame in range(frames):
-                for block in range(count):
-                    outward.append(
-                        pltpu.make_async_copy(
-                            held.at[pl.ds(low, stage), frame, pl.ds(block * per, per)],
-                            o_hbm.at[frame, pl.ds((first + block) * owners + low, stage)],
-                            leaving.at[len(outward)],
-                        )
-                    )
-                    outward[-1].start()
-        for copy in outward:
+        for copy in copies:
             copy.wait()
 
     operands = [piece]
+    in_specs = [pl.BlockSpec(memory_space=pltpu.VMEM)]
     aliases = {}
     if into is not None:
         operands.append(into)
+        in_specs.append(pl.BlockSpec(memory_space=pl.ANY))
         aliases = {1: 0}
     return pl.pallas_call(
         place_kernel,
         out_shape=jax.ShapeDtypeStruct((frames, BLOCKS * owners, per, features), jnp.bfloat16),
-        in_specs=[pl.BlockSpec(memory_space=pl.ANY)] * len(operands),
+        in_specs=in_specs,
         out_specs=pl.BlockSpec(memory_space=pl.ANY),
-        scratch_shapes=[
-            pltpu.VMEM(piece.shape, jnp.bfloat16),
-            pltpu.SemaphoreType.DMA((4,)),
-            pltpu.SemaphoreType.DMA((4 * frames * count,)),
-        ],
+        scratch_shapes=[pltpu.SemaphoreType.DMA((frames, count))],
         input_output_aliases=aliases,
-        compiler_params=pltpu.CompilerParams(vmem_limit_bytes=VMEM_LIMIT),
+        compiler_params=pltpu.CompilerParams(vmem_limit_bytes=PLACE_LIMIT),
         cost_estimate=pl.CostEstimate(
             flops=0, bytes_accessed=4 * piece.size, transcendentals=0
         ),

time: 277 us -> 275 us (level)
  no operation moved by 1% of the time
where the time goes in v2:
time: 275 us
  Pallas kernels  164 us (60%)
  waiting for transfers between devices  82.1 us (30%)
  starting transfers between devices  28.4 us (10%)
    all_to_all x5, waiting for transfers between devices, exchange(): lax.all_to_all(pieces, 'wide', split_axis=0, concat_axis=0, tiled=True)  82.1 us
    pallas_call x2, Pallas kernels, attend_time(): pl.pallas_call(functools.partial(time_kernel, sources), out_shape=jax.Sha...  74.1 us
    pallas_call x2, Pallas kernels, open_space(): pl.pallas_call(functools.partial(open_space_kernel, frame, blocks), out_s...  56.2 us
    pallas_call x1, Pallas kernels, attend_space(): pl.pallas_call(attend_space_kernel, out_shape=jax.ShapeDtypeStruct((devic...  29.2 us
    all_to_all x5, starting transfers between devices, exchange(): lax.all_to_all(pieces, 'wide', split_axis=0, concat_axis=0, tiled=True)  28.4 us
  transfers between devices with their start and end apart: 5, of which 3 were waited for; matrix products, arithmetic and copies ran while one was open for 0% of the time, Pallas kernels for 49%

profile of v2, /device:TPU:13, one launch (start us, length us, event | category | flops | bytes accessed | tf_op | source)
XLA Modules:
  0.0 274.8 jit_solution(13058109781046309986)
XLA Ops:
  0.0 28.0 %space_open.2 = (bf16[16,2,16,1152]{3,2,1,0:T(8,128)(2,1)}, bf16[2048,3456]{1,0:T(8,128)(2,1)}) custom-call(bf16[2,1024,1152]{2,1,0:T(8,128)(2,1)} %x_ref.5, f32[6,1152]{1,0:T(8,128)} %mod_ref.9, bf16[1152,3456]{1,0:T(8,128)(2,1)} %wi_ref.5, bf16[1152,1152]{1,0:T(8,128)(2,1)} %w_ref.1), custom_call_target="tpu_custom_call" | custom-call | flops 18102616064 | bytes 22413312 | tf_op jit(solution)/shard_map/space_open/pallas_call | solution.py:170
  28.0 6.6 %all-to-all-start = ((bf16[16,2,16,1152]{3,2,1,0:T(8,128)(2,1)}), bf16[16,2,16,1152]{3,2,1,0:T(8,128)(2,1)}, u32[]{:S(2)}, u32[]{:S(2)}) async-start(bf16[16,2,16,1152]{3,2,1,0:T(8,128)(2,1)} %get-tuple-element.20), calls=%async_computation | async-start | bytes 2359296 | tf_op jit(solution)/shard_map/all_to_all | solution.py:422
  34.6 28.1 %space_open.3 = (bf16[16,2,16,1152]{3,2,1,0:T(8,128)(2,1)}, bf16[2048,3456]{1,0:T(8,128)(2,1)}) custom-call(bf16[2,1024,1152]{2,1,0:T(8,128)(2,1)} %x_ref.5, f32[6,1152]{1,0:T(8,128)} %mod_ref.9, bf16[1152,3456]{1,0:T(8,128)(2,1)} %wi_ref.5, bf16[1152,1152]{1,0:T(8,128)(2,1)} %w_ref.1, ...), custom_call_target="tpu_custom_call", output_to_operand_aliasing={{1}: (4, {})} | custom-call | flops 18102616064 | bytes 22413312 | tf_op jit(solution)/shard_map/space_open/pallas_call | solution.py:170
  62.7 0.0 all-to-all-done.rest_0_
  62.7 6.0 %all-to-all-start.1 = ((bf16[16,2,16,1152]{3,2,1,0:T(8,128)(2,1)}), bf16[16,2,16,1152]{3,2,1,0:T(8,128)(2,1)}, u32[]{:S(2)}, u32[]{:S(2)}) async-start(bf16[16,2,16,1152]{3,2,1,0:T(8,128)(2,1)} %get-tuple-element.24), calls=%async_computation.1 | async-start | bytes 2359296 | tf_op jit(solution)/shard_map/all_to_all | solution.py:422
  68.8 29.2 %space_attend.1 = bf16[16,4,16,1152]{3,2,1,0:T(8,128)(2,1)} custom-call(bf16[2,1024,1152]{2,1,0:T(8,128)(2,1)} %x_ref.5, bf16[2048,3456]{1,0:T(8,128)(2,1)} %get-tuple-element.22.q_ref.k_ref.v_ref, bf16[2048,3456]{1,0:T(8,128)(2,1)} %get-tuple-element.22.q_ref.k_ref.v_ref, bf16[2048,3456]{1,0:T(8,128)(2,1)} %get-tuple-element.22.q_ref.k_ref.v_ref, ...), custom_call_target="tpu_custom_call" | custom-call | flops 19897778176 | bytes 14450688 | tf_op jit(solution)/shard_map/space_attend/pallas_call | solution.py:227
  98.0 0.0 all-to-all-done.1.rest_1_
  98.0 6.0 %all-to-all-start.2 = ((bf16[16,4,16,1152]{3,2,1,0:T(8,128)(2,1)}), bf16[16,4,16,1152]{3,2,1,0:T(8,128)(2,1)}, u32[]{:S(2)}, u32[]{:S(2)}) async-start(bf16[16,4,16,1152]{3,2,1,0:T(8,128)(2,1)} %space_attend.1), calls=%async_computation.2 | async-start | bytes 4718592 | tf_op jit(solution)/shard_map/all_to_all | solution.py:422
  104.0 37.0 %time_block.2 = bf16[16,2,32,1152]{3,2,1,0:T(8,128)(2,1)} custom-call(f32[6,1152]{1,0:T(8,128)} %mod_ref.9, bf16[1152,3456]{1,0:T(8,128)(2,1)} %wi_ref.7, bf16[1152,1152]{1,0:T(8,128)(2,1)} %wo_ref.3, bf16[16,2,16,1152]{3,2,1,0:T(8,128)(2,1)} %all-to-all-done.rest_0_, bf16[16,2,16,1152]{3,2,1,0:T(8,128)(2,1)} %all-to-all-done.1.rest_1_), custom_call_target="tpu_custom_call" | custom-call | flops 15166603264 | bytes 15335424 | tf_op jit(solution)/shard_map/time_block/pallas_call | solution.py:350
  141.1 16.1 %all-to-all-done.2.rest_0_.rest_1_ = bf16[16,4,16,1152]{3,2,1,0:T(8,128)(2,1)} async-done(((bf16[16,4,16,1152]{3,2,1,0:T(8,128)(2,1)}), bf16[16,4,16,1152]{3,2,1,0:T(8,128)(2,1)}, u32[]{:S(2)}, u32[]{:S(2)}) %all-to-all-start.2) | async-done | bytes 2359328 | tf_op jit(solution)/shard_map/all_to_all | solution.py:422
  157.2 4.9 %all-to-all-start.3 = ((bf16[16,2,32,1152]{3,2,1,0:T(8,128)(2,1)}), bf16[16,2,32,1152]{3,2,1,0:T(8,128)(2,1)}, u32[]{:S(2)}, u32[]{:S(2)}) async-start(bf16[16,2,32,1152]{3,2,1,0:T(8,128)(2,1)} %time_block.2), calls=%async_computation.3 | async-start | bytes 4718592 | tf_op jit(solution)/shard_map/all_to_all | solution.py:422
  162.1 37.0 %time_block.3 = bf16[16,2,32,1152]{3,2,1,0:T(8,128)(2,1)} custom-call(f32[6,1152]{1,0:T(8,128)} %mod_ref.9, bf16[1152,3456]{1,0:T(8,128)(2,1)} %wi_ref.7, bf16[1152,1152]{1,0:T(8,128)(2,1)} %wo_ref.3, bf16[16,4,16,1152]{3,2,1,0:T(8,128)(2,1)} %all-to-all-done.2.rest_0_.rest_1_, bf16[16,4,16,1152]{3,2,1,0:T(8,128)(2,1)} %all-to-all-done.2.rest_0_.rest_1_), custom_call_target="tpu_custom_call" | custom-call | flops 15166603264 | bytes 15335424 | tf_op jit(solution)/shard_map/time_block/pallas_call | solution.py:350
  199.1 16.1 %all-to-all-done.3.x_ref = bf16[16,2,32,1152]{3,2,1,0:T(8,128)(2,1)} async-done(((bf16[16,2,32,1152]{3,2,1,0:T(8,128)(2,1)}), bf16[16,2,32,1152]{3,2,1,0:T(8,128)(2,1)}, u32[]{:S(2)}, u32[]{:S(2)}) %all-to-all-start.3) | async-done | bytes 2359328 | tf_op jit(solution)/shard_map/all_to_all | solution.py:422
  215.2 4.9 %all-to-all-start.4 = ((bf16[16,2,32,1152]{3,2,1,0:T(8,128)(2,1)}), bf16[16,2,32,1152]{3,2,1,0:T(8,128)(2,1)S(1)}, u32[]{:S(2)}, u32[]{:S(2)}) async-start(bf16[16,2,32,1152]{3,2,1,0:T(8,128)(2,1)} %time_block.3), calls=%async_computation.4 | async-start | bytes 4718592 | tf_op jit(solution)/shard_map/all_to_all | solution.py:422
  220.1 3.1 %place_sites.2.rest_0_ = bf16[2,64,16,1152]{3,2,1,0:T(8,128)(2,1)} custom-call(bf16[16,2,32,1152]{3,2,1,0:T(8,128)(2,1)} %all-to-all-done.3.x_ref), custom_call_target="tpu_custom_call" | custom-call | bytes 4718592 | tf_op jit(solution)/shard_map/place_sites/pallas_call | solution.py:404
  223.2 49.9 %all-to-all-done.4.x_ref = bf16[16,2,32,1152]{3,2,1,0:T(8,128)(2,1)S(1)} async-done(((bf16[16,2,32,1152]{3,2,1,0:T(8,128)(2,1)}), bf16[16,2,32,1152]{3,2,1,0:T(8,128)(2,1)S(1)}, u32[]{:S(2)}, u32[]{:S(2)}) %all-to-all-start.4) | async-done | bytes 2359328 | tf_op jit(solution)/shard_map/all_to_all | solution.py:422
  273.2 1.4 place_sites.3
Async XLA Ops:
  28.0 34.7 %all-to-all-start = ((bf16[16,2,16,1152]{3,2,1,0:T(8,128)(2,1)}), bf16[16,2,16,1152]{3,2,1,0:T(8,128)(2,1)}, u32[]{:S(2)}, u32[]{:S(2)}) async-start(bf16[16,2,16,1152]{3,2,1,0:T(8,128)(2,1)} %get-tuple-element.20), calls=%async_computation | async-start | bytes 2359296 | tf_op jit(solution)/shard_map/all_to_all | solution.py:422
  62.7 35.3 %all-to-all-start.1 = ((bf16[16,2,16,1152]{3,2,1,0:T(8,128)(2,1)}), bf16[16,2,16,1152]{3,2,1,0:T(8,128)(2,1)}, u32[]{:S(2)}, u32[]{:S(2)}) async-start(bf16[16,2,16,1152]{3,2,1,0:T(8,128)(2,1)} %get-tuple-element.24), calls=%async_computation.1 | async-start | bytes 2359296 | tf_op jit(solution)/shard_map/all_to_all | solution.py:422
  98.0 59.2 %all-to-all-start.2 = ((bf16[16,4,16,1152]{3,2,1,0:T(8,128)(2,1)}), bf16[16,4,16,1152]{3,2,1,0:T(8,128)(2,1)}, u32[]{:S(2)}, u32[]{:S(2)}) async-start(bf16[16,4,16,1152]{3,2,1,0:T(8,128)(2,1)} %space_attend.1), calls=%async_computation.2 | async-start | bytes 4718592 | tf_op jit(solution)/shard_map/all_to_all | solution.py:422
  157.2 58.1 %all-to-all-start.3 = ((bf16[16,2,32,1152]{3,2,1,0:T(8,128)(2,1)}), bf16[16,2,32,1152]{3,2,1,0:T(8,128)(2,1)}, u32[]{:S(2)}, u32[]{:S(2)}) async-start(bf16[16,2,32,1152]{3,2,1,0:T(8,128)(2,1)} %time_block.2), calls=%async_computation.3 | async-start | bytes 4718592 | tf_op jit(solution)/shard_map/all_to_all | solution.py:422
  215.2 57.9 %all-to-all-start.4 = ((bf16[16,2,32,1152]{3,2,1,0:T(8,128)(2,1)}), bf16[16,2,32,1152]{3,2,1,0:T(8,128)(2,1)S(1)}, u32[]{:S(2)}, u32[]{:S(2)}) async-start(bf16[16,2,32,1152]{3,2,1,0:T(8,128)(2,1)} %time_block.3), calls=%async_computation.4 | async-start | bytes 4718592 | tf_op jit(solution)/shard_map/all_to_all | solution.py:422

commit v3 on v2

--- a/solution.py
+++ b/solution.py
@@ -419,7 +419,9 @@
 def exchange(pieces, earlier):
     if earlier is not None:
         pieces, earlier = lax.optimization_barrier((pieces, earlier))
-    return lax.all_to_all(pieces, "wide", split_axis=0, concat_axis=0, tiled=True), earlier
+    flat = pieces.reshape(pieces.shape[0], -1, pieces.shape[-1])
+    landed = lax.all_to_all(flat, "wide", split_axis=0, concat_axis=0, tiled=True)
+    return landed.reshape(pieces.shape), earlier
 
 
 def on_device(video, modulation, spatial_input, spatial_output, temporal_input, temporal_output):

time: 275 us -> 275 us (level)
  no operation moved by 1% of the time
where the time goes in v3:
time: 275 us
  Pallas kernels  164 us (60%)
  waiting for transfers between devices  82.1 us (30%)
  starting transfers between devices  28.4 us (10%)
    all_to_all x5, waiting for transfers between devices, exchange(): lax.all_to_all(flat, 'wide', split_axis=0, concat_axis=0, tiled=True)  82.1 us
    pallas_call x2, Pallas kernels, attend_time(): pl.pallas_call(functools.partial(time_kernel, sources), out_shape=jax.Sha...  74.1 us
    pallas_call x2, Pallas kernels, open_space(): pl.pallas_call(functools.partial(open_space_kernel, frame, blocks), out_s...  56.2 us
    pallas_call x1, Pallas kernels, attend_space(): pl.pallas_call(attend_space_kernel, out_shape=jax.ShapeDtypeStruct((devic...  29.2 us
    all_to_all x5, starting transfers between devices, exchange(): lax.all_to_all(flat, 'wide', split_axis=0, concat_axis=0, tiled=True)  28.4 us
  transfers between devices with their start and end apart: 5, of which 3 were waited for; matrix products, arithmetic and copies ran while one was open for 0% of the time, Pallas kernels for 49%

profile of v3, /device:TPU:13, one launch (start us, length us, event | category | flops | bytes accessed | tf_op | source)
XLA Modules:
  0.0 274.8 jit_solution(3990218199644994323)
XLA Ops:
  0.0 28.0 %space_open.2 = (bf16[16,2,16,1152]{3,2,1,0:T(8,128)(2,1)}, bf16[2048,3456]{1,0:T(8,128)(2,1)}) custom-call(bf16[2,1024,1152]{2,1,0:T(8,128)(2,1)} %x_ref.5, f32[6,1152]{1,0:T(8,128)} %mod_ref.9, bf16[1152,3456]{1,0:T(8,128)(2,1)} %wi_ref.5, bf16[1152,1152]{1,0:T(8,128)(2,1)} %w_ref.1), custom_call_target="tpu_custom_call" | custom-call | flops 18102616064 | bytes 22413312 | tf_op jit(solution)/shard_map/space_open/pallas_call | solution.py:170
  28.0 6.6 %all-to-all-start = ((bf16[16,32,1152]{2,1,0:T(8,128)(2,1)}), bf16[16,32,1152]{2,1,0:T(8,128)(2,1)}, u32[]{:S(2)}, u32[]{:S(2)}) async-start(bf16[16,32,1152]{2,1,0:T(8,128)(2,1)} %bitcast.16), calls=%async_computation | async-start | bytes 2359296 | tf_op jit(solution)/shard_map/all_to_all | solution.py:423
  34.6 28.1 %space_open.3 = (bf16[16,2,16,1152]{3,2,1,0:T(8,128)(2,1)}, bf16[2048,3456]{1,0:T(8,128)(2,1)}) custom-call(bf16[2,1024,1152]{2,1,0:T(8,128)(2,1)} %x_ref.5, f32[6,1152]{1,0:T(8,128)} %mod_ref.9, bf16[1152,3456]{1,0:T(8,128)(2,1)} %wi_ref.5, bf16[1152,1152]{1,0:T(8,128)(2,1)} %w_ref.1, ...), custom_call_target="tpu_custom_call", output_to_operand_aliasing={{1}: (4, {})} | custom-call | flops 18102616064 | bytes 22413312 | tf_op jit(solution)/shard_map/space_open/pallas_call | solution.py:170
  62.7 0.0 all-to-all-done
  62.7 6.0 %all-to-all-start.1 = ((bf16[16,32,1152]{2,1,0:T(8,128)(2,1)}), bf16[16,32,1152]{2,1,0:T(8,128)(2,1)}, u32[]{:S(2)}, u32[]{:S(2)}) async-start(bf16[16,32,1152]{2,1,0:T(8,128)(2,1)} %bitcast.15), calls=%async_computation.1 | async-start | bytes 2359296 | tf_op jit(solution)/shard_map/all_to_all | solution.py:423
  68.8 29.2 %space_attend.1 = bf16[16,4,16,1152]{3,2,1,0:T(8,128)(2,1)} custom-call(bf16[2,1024,1152]{2,1,0:T(8,128)(2,1)} %x_ref.5, bf16[2048,3456]{1,0:T(8,128)(2,1)} %get-tuple-element.22.q_ref.k_ref.v_ref, bf16[2048,3456]{1,0:T(8,128)(2,1)} %get-tuple-element.22.q_ref.k_ref.v_ref, bf16[2048,3456]{1,0:T(8,128)(2,1)} %get-tuple-element.22.q_ref.k_ref.v_ref, ...), custom_call_target="tpu_custom_call" | custom-call | flops 19897778176 | bytes 14450688 | tf_op jit(solution)/shard_map/space_attend/pallas_call | solution.py:227
  98.0 0.0 all-to-all-done.1
  98.0 6.0 %all-to-all-start.2 = ((bf16[16,64,1152]{2,1,0:T(8,128)(2,1)}), bf16[16,64,1152]{2,1,0:T(8,128)(2,1)}, u32[]{:S(2)}, u32[]{:S(2)}) async-start(bf16[16,64,1152]{2,1,0:T(8,128)(2,1)} %bitcast.12), calls=%async_computation.2 | async-start | bytes 4718592 | tf_op jit(solution)/shard_map/all_to_all | solution.py:423
  104.0 37.0 %time_block.2 = bf16[16,2,32,1152]{3,2,1,0:T(8,128)(2,1)} custom-call(f32[6,1152]{1,0:T(8,128)} %mod_ref.9, bf16[1152,3456]{1,0:T(8,128)(2,1)} %wi_ref.7, bf16[1152,1152]{1,0:T(8,128)(2,1)} %wo_ref.3, bf16[16,2,16,1152]{3,2,1,0:T(8,128)(2,1)} %bitcast.1.rest_0_, bf16[16,2,16,1152]{3,2,1,0:T(8,128)(2,1)} %bitcast.3.rest_1_), custom_call_target="tpu_custom_call" | custom-call | flops 15166603264 | bytes 15335424 | tf_op jit(solution)/shard_map/time_block/pallas_call | solution.py:350
  141.1 16.1 %all-to-all-done.2 = bf16[16,64,1152]{2,1,0:T(8,128)(2,1)} async-done(((bf16[16,64,1152]{2,1,0:T(8,128)(2,1)}), bf16[16,64,1152]{2,1,0:T(8,128)(2,1)}, u32[]{:S(2)}, u32[]{:S(2)}) %all-to-all-start.2) | async-done | bytes 2359328 | tf_op jit(solution)/shard_map/all_to_all | solution.py:423
  157.2 4.9 %all-to-all-start.3 = ((bf16[16,64,1152]{2,1,0:T(8,128)(2,1)}), bf16[16,64,1152]{2,1,0:T(8,128)(2,1)}, u32[]{:S(2)}, u32[]{:S(2)}) async-start(bf16[16,64,1152]{2,1,0:T(8,128)(2,1)} %bitcast.13), calls=%async_computation.3 | async-start | bytes 4718592 | tf_op jit(solution)/shard_map/all_to_all | solution.py:423
  162.1 37.0 %time_block.3 = bf16[16,2,32,1152]{3,2,1,0:T(8,128)(2,1)} custom-call(f32[6,1152]{1,0:T(8,128)} %mod_ref.9, bf16[1152,3456]{1,0:T(8,128)(2,1)} %wi_ref.7, bf16[1152,1152]{1,0:T(8,128)(2,1)} %wo_ref.3, bf16[16,4,16,1152]{3,2,1,0:T(8,128)(2,1)} %bitcast.5.rest_0_.rest_1_, bf16[16,4,16,1152]{3,2,1,0:T(8,128)(2,1)} %bitcast.5.rest_0_.rest_1_), custom_call_target="tpu_custom_call" | custom-call | flops 15166603264 | bytes 15335424 | tf_op jit(solution)/shard_map/time_block/pallas_call | solution.py:350
  199.1 16.1 %all-to-all-done.3 = bf16[16,64,1152]{2,1,0:T(8,128)(2,1)} async-done(((bf16[16,64,1152]{2,1,0:T(8,128)(2,1)}), bf16[16,64,1152]{2,1,0:T(8,128)(2,1)}, u32[]{:S(2)}, u32[]{:S(2)}) %all-to-all-start.3) | async-done | bytes 2359328 | tf_op jit(solution)/shard_map/all_to_all | solution.py:423
  215.2 4.9 %all-to-all-start.4 = ((bf16[16,64,1152]{2,1,0:T(8,128)(2,1)}), bf16[16,64,1152]{2,1,0:T(8,128)(2,1)S(1)}, u32[]{:S(2)}, u32[]{:S(2)}) async-start(bf16[16,64,1152]{2,1,0:T(8,128)(2,1)} %bitcast.14), calls=%async_computation.4 | async-start | bytes 4718592 | tf_op jit(solution)/shard_map/all_to_all | solution.py:423
  220.1 3.1 %place_sites.2.rest_0_ = bf16[2,64,16,1152]{3,2,1,0:T(8,128)(2,1)} custom-call(bf16[16,2,32,1152]{3,2,1,0:T(8,128)(2,1)} %bitcast.7.x_ref), custom_call_target="tpu_custom_call" | custom-call | bytes 4718592 | tf_op jit(solution)/shard_map/place_sites/pallas_call | solution.py:404
  223.2 49.9 %all-to-all-done.4 = bf16[16,64,1152]{2,1,0:T(8,128)(2,1)S(1)} async-done(((bf16[16,64,1152]{2,1,0:T(8,128)(2,1)}), bf16[16,64,1152]{2,1,0:T(8,128)(2,1)S(1)}, u32[]{:S(2)}, u32[]{:S(2)}) %all-to-all-start.4) | async-done | bytes 2359328 | tf_op jit(solution)/shard_map/all_to_all | solution.py:423
  273.2 1.4 place_sites.3
Async XLA Ops:
  28.0 34.7 %all-to-all-start = ((bf16[16,32,1152]{2,1,0:T(8,128)(2,1)}), bf16[16,32,1152]{2,1,0:T(8,128)(2,1)}, u32[]{:S(2)}, u32[]{:S(2)}) async-start(bf16[16,32,1152]{2,1,0:T(8,128)(2,1)} %bitcast.16), calls=%async_computation | async-start | bytes 2359296 | tf_op jit(solution)/shard_map/all_to_all | solution.py:423
  62.7 35.3 %all-to-all-start.1 = ((bf16[16,32,1152]{2,1,0:T(8,128)(2,1)}), bf16[16,32,1152]{2,1,0:T(8,128)(2,1)}, u32[]{:S(2)}, u32[]{:S(2)}) async-start(bf16[16,32,1152]{2,1,0:T(8,128)(2,1)} %bitcast.15), calls=%async_computation.1 | async-start | bytes 2359296 | tf_op jit(solution)/shard_map/all_to_all | solution.py:423
  98.0 59.2 %all-to-all-start.2 = ((bf16[16,64,1152]{2,1,0:T(8,128)(2,1)}), bf16[16,64,1152]{2,1,0:T(8,128)(2,1)}, u32[]{:S(2)}, u32[]{:S(2)}) async-start(bf16[16,64,1152]{2,1,0:T(8,128)(2,1)} %bitcast.12), calls=%async_computation.2 | async-start | bytes 4718592 | tf_op jit(solution)/shard_map/all_to_all | solution.py:423
  157.2 58.1 %all-to-all-start.3 = ((bf16[16,64,1152]{2,1,0:T(8,128)(2,1)}), bf16[16,64,1152]{2,1,0:T(8,128)(2,1)}, u32[]{:S(2)}, u32[]{:S(2)}) async-start(bf16[16,64,1152]{2,1,0:T(8,128)(2,1)} %bitcast.13), calls=%async_computation.3 | async-start | bytes 4718592 | tf_op jit(solution)/shard_map/all_to_all | solution.py:423
  215.2 57.9 %all-to-all-start.4 = ((bf16[16,64,1152]{2,1,0:T(8,128)(2,1)}), bf16[16,64,1152]{2,1,0:T(8,128)(2,1)S(1)}, u32[]{:S(2)}, u32[]{:S(2)}) async-start(bf16[16,64,1152]{2,1,0:T(8,128)(2,1)} %bitcast.14), calls=%async_computation.4 | async-start | bytes 4718592 | tf_op jit(solution)/shard_map/all_to_all | solution.py:423
